TPU v7x, 128 devices: a whole 4x4x4 slice. The times are simulated.
128 devices in a mesh: ctx: 16 (over y, x), exp: 8 (over z, core).
Axes of the slice: x: 4, y: 4, z: 4, core: 2. Of those that a mesh axis runs over, the one named last changes fastest.
Arguments:
- queries: bfloat16 [4, 1024, 8192], P(None, 'ctx', 'exp'), may hold values from -2 to 2
- keys: bfloat16 [4, 1024, 8192], P(None, 'ctx', 'exp'), may hold values from -2 to 2
- values: bfloat16 [4, 1024, 8192], P(None, 'ctx', 'exp'), may hold values from -6 to 6
- decay_log: float32 [1024, 64], P('ctx', 'exp'), may hold values from -0.9 to 0
- out_gate: bfloat16 [4, 1024, 8192], P(None, 'ctx', 'exp'), may hold values from -6 to 6
- head_gain: float32 [8192], P('exp'), may hold values from 0.1 to 1.9
- out_weight: bfloat16 [8192, 6144], P('exp', 'ctx'), may hold values from -0.0625 to 0.0625
- stream: bfloat16 [4, 1024, 6144], P(None, ('ctx', 'exp')), may hold values from -6 to 6
- norm_gain: float32 [6144], replicated, may hold values from 0.1 to 1.9
- expert_ids: int32 [128, 32, 2], P(('ctx', 'exp')), may hold values from 0 to 7, all different within a row; in each aligned block of 32 rows (0 to 31, 32 to 63, ..., all dimensions but the last counted through in order) at most 9 rows name the same one
- expert_share: float32 [128, 32, 2], P(('ctx', 'exp')), may hold values from 0.2 to 1
- w_gate: bfloat16 [8, 6144, 9216], P('exp', None, 'ctx'), may hold values from -0.078125 to 0.078125
- w_up: bfloat16 [8, 6144, 9216], P('exp', None, 'ctx'), may hold values from -0.078125 to 0.078125
- w_down: bfloat16 [8, 9216, 6144], P('exp', 'ctx'), may hold values from -0.0625 to 0.0625
Outputs:
- layer_out: bfloat16 [4, 1024, 6144], P(None, ('ctx', 'exp'))
Inputs may be any that keep to these rules, and one draw needn't show every extreme that they name: `expert_ids`: within a routing group no expert takes more than 9 copies, some group gives one expert exactly 9, and the two picks of a token differ.
All inputs are finite; a program needn't handle non-finite values.
Results may differ from a plain program's by a relative error of at most 0.02.
Values may be sent and summed in bfloat16 or wider, within the bound.
A program may use at most 192 MiB of HBM per device.

v0:
```python
import jax
import jax.numpy as jnp
from jax import lax
from jax.sharding import PartitionSpec as P


def carried_in(x, axis, join, neutral):
    place = lax.axis_index(axis)
    gathered = jax.tree.map(
        lambda a, kind: lax.all_gather(a.astype(kind), axis), x, (jnp.bfloat16, jnp.bfloat16)
    )
    state = jax.tree.map(lambda a, e: jnp.zeros_like(a) + jnp.asarray(e, a.dtype), x, neutral)

    def one(lap, state):
        return join(
            state,
            jax.tree.map(
                lambda a, own: lax.dynamic_index_in_dim(a, lap, 0, False).astype(own.dtype),
                gathered,
                x,
            ),
        )

    return lax.fori_loop(0, place, one, state)


def join_states(earlier, later):
    earlier_fade, earlier_state = earlier
    later_fade, later_state = later
    return (earlier_fade * later_fade, later_fade * earlier_state + later_state)


def body(
    queries,
    keys,
    values,
    decay_log,
    out_gate,
    head_gain,
    out_weight,
    stream,
    norm_gain,
    expert_ids,
    expert_share,
    w_gate,
    w_up,
    w_down,
):
    seq_count, block_len, head_width = queries.shape
    head_count = decay_log.shape[1]
    head_dim = head_width // head_count
    split_shape = (seq_count, block_len, head_count, head_dim)
    query_heads = queries.reshape(split_shape)
    key_heads = keys.reshape(split_shape)
    value_heads = values.reshape(split_shape)
    cumulative = jnp.cumsum(decay_log, axis=0)
    position = jnp.arange(block_len)
    causal = position[:, None] >= position[None, :]
    gap_log = cumulative[:, None, :] - cumulative[None, :, :]
    decay_grid = jnp.exp(jnp.where(causal[:, :, None], gap_log, -1e30))
    scores = jnp.einsum(
        "sihd,sjhd->sijh", query_heads, key_heads, preferred_element_type=jnp.float32
    )
    weights = (scores * decay_grid[None]).astype(jnp.bfloat16)
    within = jnp.einsum("sijh,sjhd->sihd", weights, value_heads, preferred_element_type=jnp.float32)
    block_end = cumulative[-1]
    keys_faded = jnp.exp(block_end[None, :] - cumulative)[None, :, :, None] * key_heads.astype(
        jnp.float32
    )
    local_state = jnp.einsum(
        "sjhd,sjhe->shde",
        keys_faded,
        value_heads.astype(jnp.float32),
        precision=lax.Precision.HIGHEST,
    )
    fading = jnp.broadcast_to(
        jnp.exp(block_end)[None, :, None, None], (seq_count, head_count, 1, 1)
    )
    identity = (jnp.ones_like(fading), jnp.zeros_like(local_state))
    incoming_fade, incoming = carried_in((fading, local_state), "ctx", join_states, identity)
    carried = jnp.exp(cumulative)[None, :, :, None] * jnp.einsum(
        "sihd,shde->sihe",
        query_heads.astype(jnp.float32),
        incoming,
        precision=lax.Precision.HIGHEST,
    )
    attended = within + carried
    mean_square = jnp.mean(attended * attended, axis=-1, keepdims=True)
    gate_act = jax.nn.sigmoid(out_gate.reshape(split_shape).astype(jnp.float32))
    gated = (
        attended
        * lax.rsqrt(mean_square + 1e-06)
        * head_gain.reshape(head_count, head_dim)
        * gate_act
    )
    mixed = gated.astype(jnp.bfloat16).reshape(seq_count, block_len, head_width)
    sub_len = stream.shape[1]
    model_width = stream.shape[2]
    exp_count = lax.axis_size("exp")
    tok_count = seq_count * sub_len
    ordered = (
        mixed.reshape(seq_count, exp_count, sub_len, head_width)
        .transpose(1, 0, 2, 3)
        .reshape(exp_count * tok_count, head_width)
    )
    full_weight = lax.all_gather(out_weight, "ctx", axis=1, tiled=True)
    chosen_rows = ordered
    projected = lax.psum_scatter(
        jnp.dot(chosen_rows, full_weight, preferred_element_type=jnp.float32).astype(jnp.bfloat16),
        "exp",
        scatter_dimension=0,
        tiled=True,
    ).astype(jnp.float32)
    residual_sum = stream.reshape(tok_count, model_width).astype(jnp.float32) + projected
    stream_square = jnp.mean(residual_sum * residual_sum, axis=-1, keepdims=True)
    normed = (residual_sum * lax.rsqrt(stream_square + 1e-06) * norm_gain).astype(jnp.bfloat16)
    expert_local = w_gate.shape[0]
    expert_count = expert_local * exp_count
    capacity = max(2, (2 * tok_count + expert_count - 1) // expert_count + 1)
    slot_total = expert_count * capacity
    picks = expert_ids.reshape(2 * tok_count)
    one_hot = (picks[:, None] == jnp.arange(expert_count, dtype=jnp.int32)[None, :]).astype(
        jnp.int32
    )
    ranking = jnp.sum(jnp.cumsum(one_hot, axis=0) * one_hot, axis=1) - 1
    slot_of = picks * capacity + ranking
    placing = slot_of[:, None] == jnp.arange(slot_total, dtype=jnp.int32)[None, :]
    copies = jnp.repeat(normed, 2, axis=0)
    dispatch = jnp.dot(
        placing.T.astype(jnp.bfloat16), copies, preferred_element_type=jnp.float32
    ).astype(jnp.bfloat16)
    dispatch = dispatch.reshape(exp_count, expert_local, capacity, model_width)
    received = lax.all_to_all(dispatch, "exp", split_axis=0, concat_axis=0, tiled=True)
    piece = lax.all_gather(received, "ctx", axis=0, tiled=True)
    gate_part = jnp.einsum("nemd,edh->nemh", piece, w_gate, preferred_element_type=jnp.float32)
    up_part = jnp.einsum("nemd,edh->nemh", piece, w_up, preferred_element_type=jnp.float32)
    hidden_units = (jax.nn.silu(gate_part) * up_part).astype(jnp.bfloat16)
    chosen_rows = hidden_units
    summed = lax.psum_scatter(
        jnp.einsum(
            "nemh,ehd->nemd", chosen_rows, w_down, preferred_element_type=jnp.float32
        ).astype(jnp.bfloat16),
        "ctx",
        scatter_dimension=0,
        tiled=True,
    )
    returned = lax.all_to_all(summed, "exp", split_axis=0, concat_axis=0, tiled=True).reshape(
        slot_total, model_width
    )
    weighting = jnp.where(placing, expert_share.reshape(2 * tok_count, 1), 0.0)
    weighting = jnp.sum(weighting.reshape(tok_count, 2, slot_total), axis=1)
    expert_mix = jnp.dot(weighting, returned.astype(jnp.float32), precision=lax.Precision.HIGHEST)
    result = (residual_sum + expert_mix).astype(jnp.bfloat16)
    return result.reshape(seq_count, sub_len, model_width)


def solution(mesh):
    return jax.shard_map(
        body,
        mesh=mesh,
        in_specs=(
            P(None, "ctx", "exp"),
            P(None, "ctx", "exp"),
            P(None, "ctx", "exp"),
            P("ctx", "exp"),
            P(None, "ctx", "exp"),
            P("exp"),
            P("exp", "ctx"),
            P(None, ("ctx", "exp"), None),
            P(),
            P(("ctx", "exp"), None, None),
            P(("ctx", "exp"), None, None),
            P("exp", None, "ctx"),
            P("exp", None, "ctx"),
            P("exp", "ctx", None),
        ),
        out_specs=P(None, ("ctx", "exp"), None),
        check_vma=False,
    )
```

profile of v0, /device:TPU:1, one launch (start us, length us, event | category | flops | bytes accessed | tf_op | source)
XLA Modules:
  0.0 671.2 jit_solution(6845622781889080944)
XLA Ops:
  6.5 0.8 copy.71
  7.6 4.0 convolution_convert_fusion.2
  11.7 0.7 all-gather.6.cloned.1.call-update
  14.1 34.7 %all-reduce = bf16[128]{0:T(256)(128)(2,1)S(1)} all-reduce(bf16[128]{0:T(256)(128)(2,1)S(1)} %dynamic-update-slice), channel_id=3, replica_groups=mesh['ctx'=16,'exp'=8] {'ctx'}, use_global_device_ids=true, to_apply=%add | all-reduce | flops 128 | bytes 512
  49.2 77.1 %all-gather.10.cloned.1.call-done = bf16[64,8,128,128]{3,2,1,0:T(8,128)(2,1)} async-done(((bf16[4,8,128,128]{3,2,1,0:T(8,128)(2,1)}), bf16[64,8,128,128]{3,2,1,0:T(8,128)(2,1)}) %all-gather.10.cloned.1.call-update) | async-done | bytes 16777232 | tf_op jit(solution)/shard_map/all_gather | solution.py:10
  126.5 3.2 fusion.24
  129.7 2.3 multiply_reduce_fusion
  133.0 93.8 %all-gather.6.cloned.1.call-done = bf16[1024,6144]{1,0:T(8,128)(2,1)} async-done(((bf16[1024,384]{1,0:T(8,128)(2,1)}), bf16[1024,6144]{1,0:T(8,128)(2,1)}) %all-gather.6.cloned.1.call-update) | async-done | bytes 12582928 | tf_op jit(solution)/shard_map/all_gather | solution.py:106
  226.8 9.4 %convolution_convert_fusion = bf16[256,6144]{1,0:T(8,128)(2,1)} fusion(bf16[256,1024]{1,0:T(8,128)(2,1)S(1)} %bitcast.180, bf16[1024,6144]{1,0:T(8,128)(2,1)} %all-gather.6.cloned.1.call-done), kind=kOutput, calls=%fused_computation.7 | convolution fusion | flops 3222798336 | bytes 16252928 | tf_op jit(solution)/shard_map/dot_general | solution.py:109
  237.4 31.9 %reduce-scatter.3.cloned.1.call-done = bf16[32,6144]{1,0:T(8,128)(2,1)} async-done(((bf16[256,6144]{1,0:T(8,128)(2,1)}), bf16[32,6144]{1,0:T(8,128)(2,1)}) %reduce-scatter.3.cloned.1.call-update) | async-done | bytes 393232 | tf_op jit(solution)/shard_map/reduce_scatter | solution.py:108
  269.4 1.2 multiply_reduce_fusion.1
  270.6 1.1 multiply_convert_fusion
  273.5 27.1 %all_to_all.10 = bf16[8,1,9,6144]{3,2,1,0:T(8,128)(2,1)S(1)} all-to-all(bf16[8,1,9,6144]{3,2,1,0:T(8,128)(2,1)S(1)} %bitcast.177), channel_id=1, replica_groups=mesh['ctx'=16,'exp'=8] {'exp'}, dimensions={0} | all-to-all | bytes 1769472 | tf_op jit(solution)/shard_map/all_to_all | solution.py:133
  300.6 1.5 copy.87
  302.3 97.3 %all-gather.8.cloned.1.call-done = bf16[128,1,9,6144]{3,0,2,1:T(8,128)(2,1)} async-done(((bf16[8,1,9,6144]{3,0,2,1:T(8,128)(2,1)}), bf16[128,1,9,6144]{3,0,2,1:T(8,128)(2,1)}) %all-gather.8.cloned.1.call-update) | async-done | bytes 14155792 | tf_op jit(solution)/shard_map/all_gather | solution.py:134
  399.6 13.7 %fusion = f32[128,9,576]{0,2,1:T(8,128)S(1)} fusion(bf16[128,1,9,6144]{3,0,2,1:T(8,128)(2,1)} %all-gather.8.cloned.1.call-done, bf16[1,6144,576]{1,2,0:T(8,128)(2,1)} %param.28), kind=kOutput, calls=%fused_computation.2 | convolution fusion | flops 8153726976 | bytes 23887872 | tf_op jit(solution)/shard_map/nemd,edh->nemh/dot_general | solution.py:136
  413.4 12.1 %fusion.17 = bf16[128,9,576]{0,2,1:T(8,128)(2,1)S(1)} fusion(f32[128,9,576]{0,2,1:T(8,128)S(1)} %fusion, bf16[1,6144,576]{1,2,0:T(8,128)(2,1)} %param.27, bf16[128,1,9,6144]{3,0,2,1:T(8,128)(2,1)S(1)} %copy-done.10), kind=kOutput, calls=%fused_computation.23 | convolution fusion | flops 8157708288 | bytes 25214976 | tf_op jit(solution)/shard_map/nemd,edh->nemh/dot_general | solution.py:135
  425.5 14.1 %convert_bitcast_fusion = bf16[128,1,9,6144]{3,0,2,1:T(8,128)(2,1)} fusion(bf16[128,9,576]{0,2,1:T(8,128)(2,1)S(1)} %fusion.17, bf16[1,576,6144]{2,1,0:T(8,128)(2,1)S(1)} %bitcast.184), kind=kOutput, calls=%fused_computation.6 | convolution fusion | flops 8160804864 | bytes 22560768 | tf_op jit(solution)/shard_map/nemh,ehd->nemd/dot_general | solution.py:140
  440.3 192.9 %all-reduce.4.cloned.1.call-done = bf16[128,1,9,6144]{3,0,2,1:T(8,128)(2,1)} async-done(((bf16[128,1,9,6144]{3,0,2,1:T(8,128)(2,1)}), bf16[128,1,9,6144]{3,0,2,1:T(8,128)(2,1)}) %all-reduce.4.cloned.1.call-update) | async-done | bytes 14155792
  633.2 1.2 constant_dynamic-slice_fusion
  634.4 1.7 copy.88
  636.1 5.1 all-to-all-start.1
  641.5 20.4 %all-to-all-done.1 = bf16[8,1,9,6144]{3,2,1,0:T(8,128)(2,1)S(1)} async-done(((bf16[8,1,9,6144]{3,2,1,0:T(8,128)(2,1)}), bf16[8,1,9,6144]{3,2,1,0:T(8,128)(2,1)S(1)}, u32[]{:S(2)}, u32[]{:S(2)}) %all-to-all-start.1) | async-done | bytes 884768 | tf_op jit(solution)/shard_map/all_to_all | solution.py:147
  662.4 2.3 fusion.8
  (73 shorter events, 6.7 us)
Async XLA Ops:
  6.5 1.1 copy-start
  6.5 6.0 copy-start.8
  6.5 119.7 %all-gather.10.cloned.1.call-start = ((), (), s32[]{:S(2)}) async-start(), calls=%async_computation.6 | async-start | bytes 17825792 | tf_op jit(solution)/shard_map/all_gather | solution.py:10
  11.6 215.2 %all-gather.6.cloned.1.call-start = ((), (), s32[]{:S(2)}) async-start(), calls=%async_computation.3 | async-start | bytes 13369344 | tf_op jit(solution)/shard_map/all_gather | solution.py:106
  12.4 257.0 %reduce-scatter.3.cloned.1.call-start = ((), (), s32[]{:S(2)}) async-start(), calls=%async_computation.4 | async-start | bytes 3538944 | tf_op jit(solution)/shard_map/reduce_scatter | solution.py:108
  126.5 3.2 copy-start.3
  129.7 2.3 copy-start.4
  129.7 2.3 copy-start.6
  236.2 0.7 copy-start.7
  236.2 33.2 %copy-start.2 = (bf16[4,8,6144]{2,1,0:T(8,128)(2,1)S(1)}, bf16[4,8,6144]{2,1,0:T(8,128)(2,1)}, u32[]{:S(2)}) copy-start(bf16[4,8,6144]{2,1,0:T(8,128)(2,1)} %param.23) | copy-start | bytes 1179652
  236.2 34.4 %copy-start.5 = (f32[6144]{0:T(1024)S(1)}, f32[6144]{0:T(1024)}, u32[]{:S(2)}) copy-start(f32[6144]{0:T(1024)} %param.24) | copy-start | bytes 73732
  236.2 163.4 %all-gather.8.cloned.1.call-start = ((), (), s32[]{:S(2)}) async-start(), calls=%async_computation.5 | async-start | bytes 15040512 | tf_op jit(solution)/shard_map/all_gather | solution.py:134
  302.1 331.1 %all-reduce.4.cloned.1.call-start = ((), (), s32[]{:S(2)}) async-start(), calls=%async_computation.7 | async-start | bytes 28311552
  399.6 13.7 %copy-start.10 = (bf16[128,1,9,6144]{3,0,2,1:T(8,128)(2,1)S(1)}, bf16[128,1,9,6144]{3,0,2,1:T(8,128)(2,1)}, u32[]{:S(2)}) copy-start(bf16[128,1,9,6144]{3,0,2,1:T(8,128)(2,1)} %all-gather.8.cloned.1.call-done) | copy-start | bytes 42467332
  399.6 25.9 %slice-start = ((s8[7077888]{0:T(1024)(128)(4,1)}), s8[4194304]{0:T(1024)(128)(4,1)S(1)}, s32[]{:S(2)}) async-start(s8[7077888]{0:T(1024)(128)(4,1)} %bitcast.183), calls=%async_computation.8 | async-start | bytes 8388608
  413.4 12.1 %slice-start.1 = ((s8[7077888]{0:T(1024)(128)(4,1)}), s8[2883584]{0:T(1024)(128)(4,1)S(1)}, s32[]{:S(2)}) async-start(s8[7077888]{0:T(1024)(128)(4,1)} %bitcast.183), calls=%async_computation.9 | async-start | bytes 5767168
  634.4 7.0 %copy-start.9 = (f32[1,32,2]{1,2,0:T(2,128)S(1)}, f32[1,32,2]{1,2,0:T(2,128)}, u32[]{:S(2)}) copy-start(f32[1,32,2]{1,2,0:T(2,128)} %param.26) | copy-start | bytes 772
  636.1 25.8 %all-to-all-start.1 = ((bf16[8,1,9,6144]{3,2,1,0:T(8,128)(2,1)}), bf16[8,1,9,6144]{3,2,1,0:T(8,128)(2,1)S(1)}, u32[]{:S(2)}, u32[]{:S(2)}) async-start(bf16[8,1,9,6144]{3,2,1,0:T(8,128)(2,1)} %copy.88), calls=%async_computation.2 | async-start | bytes 3145728 | tf_op jit(solution)/shard_map/all_to_all | solution.py:147
  641.2 23.4 %copy-start.1 = (bf16[4,64,1024]{2,1,0:T(8,128)(2,1)S(1)}, bf16[4,64,1024]{2,1,0:T(8,128)(2,1)}, u32[]{:S(2)}) copy-start(bf16[4,64,1024]{2,1,0:T(8,128)(2,1)} %param.18) | copy-start | bytes 1572868
Sparse Core Ops, SparseCore 0:
  11.7 114.4 all-gather.9
  128.4 98.3 all-gather.5
  236.3 32.9 reduce-scatter.2
  302.2 97.3 all-gather.7
  439.8 193.3 all-reduce.3
where the time goes:
time: 672 us; the launch traced here: 671 us
  waiting for transfers between devices  514 us (76%)
  blocking collectives  61.9 us (9%)
  matrix products  61.5 us (9%)
  between operations  14.8 us (2%)
  local copies, waits for them, and re-layouts  9.89 us (1%)
    unnamed x6, waiting for transfers between devices  194 us
    all_gather x1, waiting for transfers between devices, body(): piece = lax.all_gather(received, 'ctx', axis=0, tiled=True)  97.3 us
    all_gather x1, waiting for transfers between devices, body(): full_weight = lax.all_gather(out_weight, 'ctx', axis=1, tiled=True)  93.8 us
    all_gather x1, waiting for transfers between devices, carried_in(): lax.all_gather(a.astype(kind), axis)  77.1 us
    unnamed x1, blocking collectives  34.7 us
    reduce_scatter x1, waiting for transfers between devices, body(): lax.psum_scatter(jnp.dot(chosen_rows, full_weight, preferred_element_type...  31.9 us
    all_to_all x1, blocking collectives, body(): lax.all_to_all(dispatch, 'exp', split_axis=0, concat_axis=0, tiled=True)  27.1 us
    all_to_all x1, waiting for transfers between devices, body(): lax.all_to_all(summed, 'exp', split_axis=0, concat_axis=0, tiled=True)  20.4 us
  transfers between devices with their start and end apart: 6, of which 6 were waited for; matrix products, arithmetic and copies ran while one was open for 1% of the time, Pallas kernels for 0%

commit v1 on v0

--- a/solution.py
+++ b/solution.py
@@ -131,7 +131,10 @@
     ).astype(jnp.bfloat16)
     dispatch = dispatch.reshape(exp_count, expert_local, capacity, model_width)
     received = lax.all_to_all(dispatch, "exp", split_axis=0, concat_axis=0, tiled=True)
-    piece = lax.all_gather(received, "ctx", axis=0, tiled=True)
+    count = lax.axis_size("ctx")
+    shards = jnp.stack([received for _ in range(count)])
+    shards = lax.all_to_all(shards, "ctx", split_axis=0, concat_axis=0)
+    piece = jnp.concatenate(shards, axis=0)
     gate_part = jnp.einsum("nemd,edh->nemh", piece, w_gate, preferred_element_type=jnp.float32)
     up_part = jnp.einsum("nemd,edh->nemh", piece, w_up, preferred_element_type=jnp.float32)
     hidden_units = (jax.nn.silu(gate_part) * up_part).astype(jnp.bfloat16)

time: 672 us -> 755 us (1.12)
  blocking collectives: 61.9 us -> 225 us
  waiting for transfers between devices: 514 us -> 413 us
  local copies, waits for them, and re-layouts: 9.89 us -> 21 us
  matrix products: 61.5 us -> 70.9 us
    all_to_all x0 -> x1, blocking collectives: none -> 163 us  [body(): shards = lax.all_to_all(shards, 'ctx', split_axis=0, concat_axis=0)]
    all_gather x1 -> x0, waiting for transfers between devices: 97.3 us -> none  [body(): piece = lax.all_gather(received, 'ctx', axis=0, tiled=True)]
    dot_general x1, matrix products: 14.1 us -> 32.2 us  [body(): jnp.einsum('nemh,ehd->nemd', chosen_rows, w_down, preferred_element_type=...]
    dot_general x1 -> x0, matrix products: 12.1 us -> none  [body(): jnp.einsum('nemd,edh->nemh', piece, w_gate, preferred_element_type=jnp.fl...]
    unnamed x6 -> x5, waiting for transfers between devices: 194 us -> 191 us
  transfers between devices with their start and end apart: 6 -> 5, of which waited for: 6 -> 5; matrix products, arithmetic and copies ran while one was open for 1% -> 1% of each run, Pallas kernels for 0% -> 0%
where the time goes in v1:
time: 755 us; the launch traced here: 754 us
  waiting for transfers between devices  413 us (55%)
  blocking collectives  225 us (30%)
  matrix products  70.9 us (9%)
  local copies, waits for them, and re-layouts  21 us (3%)
  between operations  14.8 us (2%)
    unnamed x5, waiting for transfers between devices  191 us
    all_to_all x1, blocking collectives, body(): shards = lax.all_to_all(shards, 'ctx', split_axis=0, concat_axis=0)  163 us
    all_gather x1, waiting for transfers between devices, body(): full_weight = lax.all_gather(out_weight, 'ctx', axis=1, tiled=True)  92.8 us
    all_gather x1, waiting for transfers between devices, carried_in(): lax.all_gather(a.astype(kind), axis)  76.3 us
    unnamed x1, blocking collectives  34.7 us
    reduce_scatter x1, waiting for transfers between devices, body(): lax.psum_scatter(jnp.dot(chosen_rows, full_weight, preferred_element_type...  32.5 us
    dot_general x1, matrix products, body(): jnp.einsum('nemh,ehd->nemd', chosen_rows, w_down, preferred_element_type=...  32.2 us
    all_to_all x1, blocking collectives, body(): lax.all_to_all(dispatch, 'exp', split_axis=0, concat_axis=0, tiled=True)  27.1 us
  transfers between devices with their start and end apart: 5, of which 5 were waited for; matrix products, arithmetic and copies ran while one was open for 1% of the time, Pallas kernels for 0%

profile of v1, /device:TPU:1, one launch (start us, length us, event | category | flops | bytes accessed | tf_op | source)
XLA Modules:
  0.0 754.2 jit_solution(11211776098043050935)
XLA Ops:
  7.6 4.0 convolution_convert_fusion.2
  12.5 1.4 fusion.58
  14.8 34.7 %all-reduce = bf16[128]{0:T(256)(128)(2,1)S(1)} all-reduce(bf16[128]{0:T(256)(128)(2,1)S(1)} %dynamic-update-slice), channel_id=3, replica_groups=mesh['ctx'=16,'exp'=8] {'ctx'}, use_global_device_ids=true, to_apply=%add | all-reduce | flops 128 | bytes 512
  49.9 76.3 %all-gather.7.cloned.1.call-done = bf16[64,8,128,128]{3,2,1,0:T(8,128)(2,1)} async-done(((bf16[4,8,128,128]{3,2,1,0:T(8,128)(2,1)}), bf16[64,8,128,128]{3,2,1,0:T(8,128)(2,1)}) %all-gather.7.cloned.1.call-update) | async-done | bytes 16777232 | tf_op jit(solution)/shard_map/all_gather | solution.py:10
  126.5 3.2 fusion.30
  129.7 2.2 multiply_reduce_fusion
  131.9 1.4 fusion.33
  133.9 92.8 %all-gather.5.cloned.1.call-done = bf16[1024,6144]{1,0:T(8,128)(2,1)} async-done(((bf16[1024,384]{1,0:T(8,128)(2,1)}), bf16[1024,6144]{1,0:T(8,128)(2,1)}) %all-gather.5.cloned.1.call-update) | async-done | bytes 12582928 | tf_op jit(solution)/shard_map/all_gather | solution.py:106
  226.7 9.4 %convolution_convert_fusion = bf16[256,6144]{1,0:T(8,128)(2,1)} fusion(bf16[256,1024]{1,0:T(8,128)(2,1)S(1)} %bitcast.191, bf16[1024,6144]{1,0:T(8,128)(2,1)} %all-gather.5.cloned.1.call-done), kind=kOutput, calls=%fused_computation.9 | convolution fusion | flops 3222798336 | bytes 16252928 | tf_op jit(solution)/shard_map/dot_general | solution.py:109
  236.8 32.5 %reduce-scatter.3.cloned.1.call-done = bf16[32,6144]{1,0:T(8,128)(2,1)} async-done(((bf16[256,6144]{1,0:T(8,128)(2,1)}), bf16[32,6144]{1,0:T(8,128)(2,1)}) %reduce-scatter.3.cloned.1.call-update) | async-done | bytes 393232 | tf_op jit(solution)/shard_map/reduce_scatter | solution.py:108
  269.3 1.2 multiply_reduce_fusion.1
  270.6 1.2 multiply_convert_fusion
  273.4 27.1 %all_to_all.18 = bf16[8,1,9,6144]{3,2,1,0:T(8,128)(2,1)S(1)} all-to-all(bf16[8,1,9,6144]{3,2,1,0:T(8,128)(2,1)S(1)} %bitcast.187), channel_id=1, replica_groups=mesh['ctx'=16,'exp'=8] {'exp'}, dimensions={0} | all-to-all | bytes 1769472 | tf_op jit(solution)/shard_map/all_to_all | solution.py:133
  301.1 6.8 stack.2
  307.9 162.9 %all_to_all.19 = bf16[16,8,1,9,6144]{4,1,3,2,0:T(8,128)(2,1)S(1)} all-to-all(bf16[16,8,1,9,6144]{4,1,3,2,0:T(8,128)(2,1)} %stack.2), channel_id=1, replica_groups=mesh['ctx'=16,'exp'=8] {'ctx'}, dimensions={0} | all-to-all | bytes 28311552 | tf_op jit(solution)/shard_map/all_to_all | solution.py:136
  470.8 5.1 copy-done.2
  475.9 17.1 %fusion = f32[128,9,576]{0,2,1:T(8,128)} fusion(bf16[16,8,1,9,6144]{4,1,3,2,0:T(8,128)(2,1)S(1)} %all_to_all.19, bf16[1,6144,576]{1,2,0:T(8,128)(2,1)} %param.28), kind=kOutput, calls=%fused_computation.2 | convolution fusion | flops 8153726976 | bytes 23887872 | tf_op jit(solution)/shard_map/nemd,edh->nemh/dot_general | solution.py:139
  493.0 32.2 %convert_bitcast_fusion = bf16[128,1,9,6144]{3,0,2,1:T(8,128)(2,1)} fusion(bf16[1,576,6144]{2,1,0:T(8,128)(2,1)} %param.29, f32[128,9,576]{0,2,1:T(8,128)} %fusion, bf16[1,6144,576]{1,2,0:T(8,128)(2,1)} %param.27, bf16[16,8,1,9,6144]{4,1,3,2,0:T(8,128)(2,1)} %copy-done.2), kind=kOutput, calls=%fused_computation.6 | convolution fusion | flops 16318513152 | bytes 45121536 | tf_op jit(solution)/shard_map/nemh,ehd->nemd/dot_general | solution.py:143
  526.0 190.2 %all-reduce.4.cloned.1.call-done = bf16[128,1,9,6144]{3,0,2,1:T(8,128)(2,1)} async-done(((bf16[128,1,9,6144]{3,0,2,1:T(8,128)(2,1)}), bf16[128,1,9,6144]{3,0,2,1:T(8,128)(2,1)}) %all-reduce.4.cloned.1.call-update) | async-done | bytes 14155792
  716.2 1.2 constant_dynamic-slice_fusion
  717.5 1.7 copy.90
  719.2 5.1 all-to-all-start.2
  724.5 20.4 %all-to-all-done.2 = bf16[8,1,9,6144]{3,2,1,0:T(8,128)(2,1)S(1)} async-done(((bf16[8,1,9,6144]{3,2,1,0:T(8,128)(2,1)}), bf16[8,1,9,6144]{3,2,1,0:T(8,128)(2,1)S(1)}, u32[]{:S(2)}, u32[]{:S(2)}) %all-to-all-start.2) | async-done | bytes 884768 | tf_op jit(solution)/shard_map/all_to_all | solution.py:150
  745.4 2.3 fusion.10
  (62 shorter events, 6.9 us)
Async XLA Ops:
  6.5 1.1 copy-start
  6.5 119.7 %all-gather.7.cloned.1.call-start = ((), (), s32[]{:S(2)}) async-start(), calls=%async_computation.6 | async-start | bytes 17825792 | tf_op jit(solution)/shard_map/all_gather | solution.py:10
  11.6 215.1 %all-gather.5.cloned.1.call-start = ((), (), s32[]{:S(2)}) async-start(), calls=%async_computation.4 | async-start | bytes 13369344 | tf_op jit(solution)/shard_map/all_gather | solution.py:106
  12.4 257.0 %reduce-scatter.3.cloned.1.call-start = ((), (), s32[]{:S(2)}) async-start(), calls=%async_computation.5 | async-start | bytes 3538944 | tf_op jit(solution)/shard_map/reduce_scatter | solution.py:108
  126.4 3.2 copy-start.4
  126.5 5.4 copy-start.6
  226.7 9.5 %copy-start.7 = (s32[1,32,2]{1,2,0:T(2,128)S(1)}, s32[1,32,2]{1,2,0:T(2,128)}, u32[]{:S(2)}) copy-start(s32[1,32,2]{1,2,0:T(2,128)} %param.25) | copy-start | bytes 772
  226.7 42.6 %copy-start.3 = (bf16[4,8,6144]{2,1,0:T(8,128)(2,1)S(1)}, bf16[4,8,6144]{2,1,0:T(8,128)(2,1)}, u32[]{:S(2)}) copy-start(bf16[4,8,6144]{2,1,0:T(8,128)(2,1)} %param.23) | copy-start | bytes 1179652
  226.7 43.8 %copy-start.5 = (f32[6144]{0:T(1024)S(1)}, f32[6144]{0:T(1024)}, u32[]{:S(2)}) copy-start(f32[6144]{0:T(1024)} %param.24) | copy-start | bytes 73732
  236.2 480.1 %all-reduce.4.cloned.1.call-start = ((), (), s32[]{:S(2)}) async-start(), calls=%async_computation.7 | async-start | bytes 28311552
  470.8 5.1 copy-start.2
  525.3 199.2 %copy-start.8 = (f32[1,32,2]{1,2,0:T(2,128)S(1)}, f32[1,32,2]{1,2,0:T(2,128)}, u32[]{:S(2)}) copy-start(f32[1,32,2]{1,2,0:T(2,128)} %param.26) | copy-start | bytes 772
  525.3 222.4 %copy-start.1 = (bf16[4,64,1024]{2,1,0:T(8,128)(2,1)S(1)}, bf16[4,64,1024]{2,1,0:T(8,128)(2,1)}, u32[]{:S(2)}) copy-start(bf16[4,64,1024]{2,1,0:T(8,128)(2,1)} %param.18) | copy-start | bytes 1572868
  719.2 25.8 %all-to-all-start.2 = ((bf16[8,1,9,6144]{3,2,1,0:T(8,128)(2,1)}), bf16[8,1,9,6144]{3,2,1,0:T(8,128)(2,1)S(1)}, u32[]{:S(2)}, u32[]{:S(2)}) async-start(bf16[8,1,9,6144]{3,2,1,0:T(8,128)(2,1)} %copy.90), calls=%async_computation.3 | async-start | bytes 3145728 | tf_op jit(solution)/shard_map/all_to_all | solution.py:150
Sparse Core Ops, SparseCore 0:
  11.7 114.4 all-gather.6
  128.3 98.3 all-gather.4
  236.3 32.9 reduce-scatter.2
  525.4 190.8 all-reduce.3
